TPU v7x, 32 devices: a whole 2x2x4 slice. The times are simulated.
32 devices in a mesh: hyp: 2 (over y), row: 4 (over z), col: 4 (over x, core).
Axes of the slice: x: 2, y: 2, z: 4, core: 2. Of those that a mesh axis runs over, the one named last changes fastest.
Arguments:
- inverse_tile: float32 [16384, 8192], P(('hyp', 'row'), 'col'), parts along dimension 0, may hold values from -32768 to 262144, as said below
- panels: float32 [2, 2, 8192, 512], P('hyp', None, ('col', 'row')), parts along dimension 0, may hold values from -0.0007324219 to 0.0007324219
- link_panel: float32 [2, 512, 512], P('hyp'), parts along dimension 0, may hold values from -0.09375 to 0.09375
- diag_inverse: float32 [2, 2, 512, 512], P('hyp', None, 'row', 'col'), parts along dimension 0, may hold values from -3 to 3
- ancestor_tiles: int32 [1, 2, 64], replicated, may hold values 0 or 1
Outputs:
- ancestor_block: float32 [2, 2, 8192, 512], P('hyp', None, ('row', 'col')), parts along dimension 0
- diag_block: float32 [2, 2, 512, 512], P('hyp', None, 'row', 'col'), parts along dimension 0
- cross_block: float32 [2, 512, 512], P('hyp', 'row', 'col'), parts along dimension 0
There are 2 independent parts, one for each index of `hyp`. A program takes and returns all parts, laid end to end along the dimension named above; an argument that names none is the same for every part. Nothing has to cross between parts.
Inputs may be any that keep to these rules, and one draw needn't show every extreme that they name: `inverse_tile`: symmetric.
All inputs are finite; a program needn't handle non-finite values.
Results may differ from a plain program's by a relative error of at most 0.000075.
Values sent between devices are 32-bit elements; how exact they have to be, the bound alone decides.
A program may use at most 128 MiB of HBM per device.

v0:
```python
import functools

import jax
import jax.numpy as jnp
from jax import lax
from jax.experimental import pallas as pl
from jax.experimental.pallas import tpu as pltpu
from jax.sharding import PartitionSpec as P

TILE = 128
MESH = pl.DeviceIdType.MESH


def mask_panels(panels, ancestor_tiles):
    rows_axis = lax.axis_size("row")
    local_rows = panels.shape[2]
    row_start = (lax.axis_index("col") * rows_axis + lax.axis_index("row")) * local_rows
    tile_mask = jnp.repeat(ancestor_tiles, TILE, axis=2)
    kept_rows = lax.dynamic_slice_in_dim(tile_mask, row_start, local_rows, 2)
    return jnp.where(kept_rows[..., None] != 0, panels, 0.0)


def exchange(axis_sizes, chunks, a_hbm, x_hbm, y_ref, own_ref, a_hi, a_lo, stage, p_hi, p_lo, gathered, partial,
             received, own, stage_sem, load_sem, send_sem, recv_sem, part_send, part_recv, own_send, own_recv, own_local):
    rows_axis, cols_axis = axis_sizes
    r = lax.axis_index("row")
    c = lax.axis_index("col")
    _, _, rows, width = gathered.shape
    half = rows // 2
    per_panel = chunks // x_hbm.shape[0]
    pieces = 2 * (rows_axis - 1)
    tile = stage.shape[1]
    tiles = a_hbm.shape[0] // tile

    def load(q):
        src = x_hbm.at[q // per_panel, :, pl.ds((q % per_panel) * width, width)]
        return pltpu.make_async_copy(src, gathered.at[q, r], load_sem.at[q])

    def stage_copy(i):
        src = a_hbm.at[pl.ds(pl.multiple_of(i * tile, tile), tile)]
        return pltpu.make_async_copy(src, stage.at[i % 2], stage_sem.at[i % 2])

    def hop(q, block, h, way, target):
        ref = gathered.at[q, block, pl.ds(pl.multiple_of(h * half, half), half)]
        return pltpu.make_async_remote_copy(
            ref, ref, send_sem.at[way, q, block, h], recv_sem.at[q, block, h],
            device_id={"row": target}, device_id_type=MESH)

    def each_send(q, s, h, act):
        @pl.when((r + 1 < rows_axis) & (r - s >= 0))
        def _():
            act(hop(q, r - s, h, 0, r + 1))

        @pl.when((r >= 1) & (r + s < rows_axis))
        def _():
            act(hop(q, r + s, h, 1, r - 1))

    def wait_arrivals(q, s, h):
        @pl.when(r - 1 - s >= 0)
        def _():
            hop(q, r - 1 - s, h, 0, r - 1).wait_recv()

            @pl.when(h == 1)
            def _():
                own_of_block(q, r - 1 - s)

        @pl.when(r + 1 + s < rows_axis)
        def _():
            hop(q, r + 1 + s, h, 1, r + 1).wait_recv()

            @pl.when(h == 1)
            def _():
                own_of_block(q, r + 1 + s)

    def part(q, target, source):
        return pltpu.make_async_remote_copy(
            partial.at[q, target], received.at[q, source], part_send.at[q, target], part_recv.at[q, source],
            device_id={"col": target}, device_id_type=MESH)

    def own_copy(q, target):
        return pltpu.make_async_remote_copy(
            gathered.at[q, (r * cols_axis + target) % rows_axis], own.at[q], own_send.at[q, target], own_recv.at[q],
            device_id={"col": target}, device_id_type=MESH)

    def own_here(q):
        return pltpu.make_async_copy(gathered.at[q, (r * cols_axis + c) % rows_axis], own.at[q], own_local.at[q])

    own_root = (r * cols_axis + c) // rows_axis

    def own_of_block(q, block):
        for shift in range(1, cols_axis):
            target = (c + shift) % cols_axis
            place = r * cols_axis + target

            @pl.when((place // rows_axis == c) & (place % rows_axis == block))
            def _():
                own_copy(q, target).start()

    def each_own(q, act):
        for shift in range(1, cols_axis):
            target = (c + shift) % cols_axis

            @pl.when((r * cols_axis + target) // rows_axis == c)
            def _():
                act(own_copy(q, target))

    for q in range(chunks):
        load(q).start()
    stage_copy(0).start()
    barrier = pltpu.get_barrier_semaphore()
    for shift in range(1, cols_axis):
        pl.semaphore_signal(barrier, inc=1, device_id={"col": (c + shift) % cols_axis}, device_id_type=MESH)

    @pl.when(r >= 1)
    def _():
        pl.semaphore_signal(barrier, inc=1, device_id={"row": r - 1}, device_id_type=MESH)

    @pl.when(r + 1 < rows_axis)
    def _():
        pl.semaphore_signal(barrier, inc=1, device_id={"row": r + 1}, device_id_type=MESH)

    inner = (r >= 1) & (r + 1 < rows_axis)

    @pl.when(inner)
    def _():
        pl.semaphore_wait(barrier, cols_axis + 1)

    @pl.when(jnp.logical_not(inner))
    def _():
        pl.semaphore_wait(barrier, cols_axis)

    for q in range(chunks):
        load(q).wait()

    def split_tile(i, carry):
        @pl.when(i + 1 < tiles)
        def _():
            stage_copy(i + 1).start()

        stage_copy(i).wait()
        at = pl.ds(pl.multiple_of(i * tile, tile), tile)
        value = stage[i % 2]
        high = value.astype(jnp.bfloat16)
        a_hi[at, :] = high
        a_lo[at, :] = (value - high.astype(jnp.float32)).astype(jnp.bfloat16)
        return carry

    def multiply(k, i):
        even = 1 - 2 * (c % 2)
        target = (c + cols_axis // 2 + even * i + cols_axis) % cols_axis
        at = pl.ds(pl.multiple_of(target * rows, rows), rows)
        high = a_hi[at, :]
        out = jnp.dot(high, p_hi[...], preferred_element_type=jnp.float32)
        out += jnp.dot(high, p_lo[...], preferred_element_type=jnp.float32)
        out += jnp.dot(a_lo[at, :], p_hi[...], preferred_element_type=jnp.float32)
        partial[k, target] = out

        @pl.when(target != c)
        def _():
            part(k, target, c).start()

    def step(u, carry):
        q, p = u // pieces, u % pieces
        s, h = p // 2, p % 2

        @pl.when((u >= 2) & (u < chunks * pieces + 2))
        def _():
            v = u - 2
            wait_arrivals(v // pieces, (v % pieces) // 2, v % 2)

        @pl.when(q < chunks)
        def _():
            each_send(q, s, h, lambda copy: copy.start())

        @pl.when((q < chunks) & (p == 0))
        def _():
            own_of_block(q, r)

        @pl.when(u == 1)
        def _():
            lax.fori_loop(0, tiles, split_tile, 0)

        @pl.when((q >= 1) & (p == 1))
        def _():
            k = q - 1

            @pl.when(own_root == c)
            def _():
                own_here(k).start()

            def split_panel(b, carry):
                at = pl.ds(pl.multiple_of(b * rows, rows), rows)
                value = gathered[k, b]
                high = value.astype(jnp.bfloat16)
                p_hi[at, :] = high
                p_lo[at, :] = (value - high.astype(jnp.float32)).astype(jnp.bfloat16)
                return carry

            lax.fori_loop(0, rows_axis, split_panel, 0)

        @pl.when((q >= 1) & (p >= 1))
        def _():
            def body(i, carry):
                multiply(q - 1, i)
                return carry

            lax.fori_loop((p - 1) * cols_axis // (pieces - 1), p * cols_axis // (pieces - 1), body, 0)

        return carry

    lax.fori_loop(0, (chunks + 1) * pieces, step, 0)

    for q in range(chunks):
        panel, start = q // per_panel, (q % per_panel) * width
        at = (panel, slice(None), slice(start, start + width))
        total = partial[q, c]
        for shift in range(1, cols_axis):
            source = (c + shift) % cols_axis
            part(q, source, source).wait_recv()
            total += received[q, source]
        y_ref[at] = total

        @pl.when(own_root == c)
        def _():
            own_here(q).wait()

        @pl.when(own_root != c)
        def _():
            own_copy(q, own_root).wait_recv()

        own_ref[at] = own[q]

    def drain(u, carry):
        q, p = u // pieces, u % pieces
        each_send(q, p // 2, p % 2, lambda copy: copy.wait_send())
        return carry

    lax.fori_loop(0, chunks * pieces, drain, 0)
    for q in range(chunks):
        each_own(q, lambda copy: copy.wait_send())
        for shift in range(1, cols_axis):
            part(q, (c + shift) % cols_axis, c).wait_send()


def products(inverse_tile, masked):
    rows_axis, cols_axis = lax.axis_size("row"), lax.axis_size("col")
    height, depth = inverse_tile.shape
    count, rows, columns = masked.shape
    width = min(256, columns)
    chunks = count * columns // width
    tile = min(128, height)
    f32, bf16 = jnp.float32, jnp.bfloat16
    dma = pltpu.SemaphoreType.DMA
    result = jax.ShapeDtypeStruct((count, rows, columns), f32)
    return pl.pallas_call(
        functools.partial(exchange, (rows_axis, cols_axis), chunks),
        out_shape=(result, result),
        in_specs=[pl.BlockSpec(memory_space=pl.ANY)] * 2,
        out_specs=[pl.BlockSpec(memory_space=pltpu.VMEM)] * 2,
        scratch_shapes=[
            pltpu.VMEM((height, depth), bf16),
            pltpu.VMEM((height, depth), bf16),
            pltpu.VMEM((2, tile, depth), f32),
            pltpu.VMEM((depth, width), bf16),
            pltpu.VMEM((depth, width), bf16),
            pltpu.VMEM((chunks, rows_axis, rows, width), f32),
            pltpu.VMEM((chunks, cols_axis, rows, width), f32),
            pltpu.VMEM((chunks, cols_axis, rows, width), f32),
            pltpu.VMEM((chunks, rows, width), f32),
            dma((2,)),
            dma((chunks,)),
            dma((2, chunks, rows_axis, 2)),
            dma((chunks, rows_axis, 2)),
            dma((chunks, cols_axis)),
            dma((chunks, cols_axis)),
            dma((chunks, cols_axis)),
            dma((chunks,)),
            dma((chunks,)),
        ],
        compiler_params=pltpu.CompilerParams(
            collective_id=0, has_side_effects=True, vmem_limit_bytes=60 * 1024 * 1024),
    )(inverse_tile, masked)


def halving_levels():
    levels = []
    for axis in ("col", "row"):
        dist = 1
        while dist < lax.axis_size(axis):
            levels.append((axis, dist))
            dist *= 2
    return levels


def split(value):
    high = value.astype(jnp.bfloat16)
    return high, (value - high.astype(jnp.float32)).astype(jnp.bfloat16)


def dot3(a, b, contract):
    def one(left, right):
        return lax.dot_general(
            left, right, (((contract,), (0,)), ((), ())), preferred_element_type=jnp.float32)

    return one(a[0], b[0]) + (one(a[0], b[1]) + one(a[1], b[0]))


def finish_kernel(levels, count, y_ref, own_ref, link_ref, given_ref, anc_ref, diag_ref, cross_ref, terms, out_ref, *scratch):
    depth = len(levels)
    height, span = given_ref.shape[1:]
    rows_axis, cols_axis = terms.shape[3], 2 * terms.shape[1]
    kept = (terms,) + scratch[: depth - 1]
    landed = scratch[depth - 1 : 2 * depth - 1]
    send_sem, recv_sem = scratch[2 * depth - 1 :]

    def bit_and_partner(level):
        axis, dist = levels[level]
        at = lax.axis_index(axis)
        bit = (at // dist) % 2
        return bit, {axis: at + dist * (1 - 2 * bit)}

    def copy(level, k):
        bit, partner = bit_and_partner(level)
        return pltpu.make_async_remote_copy(
            kept[level].at[k, :, 1 - bit], landed[level].at[k], send_sem.at[level, k], recv_sem.at[level, k],
            device_id=partner, device_id_type=MESH)

    barrier = pltpu.get_barrier_semaphore()
    for level in range(depth):
        pl.semaphore_signal(barrier, inc=1, device_id=bit_and_partner(level)[1], device_id_type=MESH)
    pl.semaphore_wait(barrier, depth)

    def store(k, value):
        for col in range(cols_axis):
            for row in range(rows_axis):
                terms[k, col // 2, col % 2, row] = value[
                    row * height : (row + 1) * height, col * span : (col + 1) * span]

    row_id, col_id = lax.axis_index("row"), lax.axis_index("col")
    y1 = -y_ref[0]
    anc_ref[0] = y1
    first, y1_parts = split(own_ref[0]), split(y1)
    store(0, dot3(first, y1_parts, 0))
    copy(0, 0).start()
    link = split(link_ref[...])
    link_cols = link_ref[pl.ds(pl.multiple_of(col_id * span, span), span), :]
    link_rows = link_ref[pl.ds(pl.multiple_of(row_id * height, height), height), :]
    given = dot3(split(given_ref[0]), split(link_cols), 1)
    y2 = -(y_ref[1] + dot3(y1_parts, link, 1))
    anc_ref[1] = y2
    y2_parts = split(y2)
    store(1, dot3(first, y2_parts, 0))
    for col in range(cols_axis):
        terms[1, col // 2, col % 2, row_id] += given[:, col * span : (col + 1) * span]
    copy(0, 1).start()
    shifted = split(own_ref[1] - dot3(first, link, 1))
    store(2, dot3(shifted, y2_parts, 0) - dot3(split(link_rows), split(given), 0))
    copy(0, 2).start()

    for level in range(1, depth + 1):
        for k in range(count):
            copy(level - 1, k).wait_recv()
            bit, _ = bit_and_partner(level - 1)
            total = kept[level - 1][k, :, bit] + landed[level - 1][k]
            target = kept[level] if level < depth else out_ref
            target[k] = total.reshape(target.shape[1:])
            if level < depth:
                copy(level, k).start()
    diag_ref[0] = given_ref[0] - out_ref[0]
    diag_ref[1] = given_ref[1] - out_ref[2]
    cross_ref[...] = -out_ref[1]
    for level in range(depth):
        for k in range(count):
            copy(level, k).wait_send()


def finish(y, own, link, given):
    rows_axis, cols_axis = lax.axis_size("row"), lax.axis_size("col")
    count = 3
    height, span = given.shape[1:]
    levels = halving_levels()
    shapes = []
    cols, rows = cols_axis, rows_axis
    for axis, _ in levels:
        if axis == "col":
            cols //= 2
            shapes.append(((cols, 2, rows, height, span), (cols, rows, height, span)))
        else:
            rows //= 2
            shapes.append(((rows, 2, height, span), (rows, height, span)))
    dma = pltpu.SemaphoreType.DMA((len(levels), count))
    return pl.pallas_call(
        functools.partial(finish_kernel, levels, count),
        out_shape=(
            jax.ShapeDtypeStruct(y.shape, jnp.float32),
            jax.ShapeDtypeStruct(given.shape, jnp.float32),
            jax.ShapeDtypeStruct((height, span), jnp.float32),
        ),
        in_specs=[pl.BlockSpec(memory_space=pltpu.VMEM)] * 4,
        out_specs=[pl.BlockSpec(memory_space=pltpu.VMEM)] * 3,
        scratch_shapes=[
            pltpu.VMEM((count,) + shapes[0][0], jnp.float32),
            pltpu.VMEM((count, height, span), jnp.float32),
        ]
        + [pltpu.VMEM((count,) + kept, jnp.float32) for kept, _ in shapes[1:]]
        + [pltpu.VMEM((count,) + landed, jnp.float32) for _, landed in shapes]
        + [dma, dma],
        compiler_params=pltpu.CompilerParams(
            collective_id=1, has_side_effects=True, vmem_limit_bytes=48 * 1024 * 1024),
    )(y, own, link, given)


def local(inverse_tile, panels, link_panel, diag_inverse, ancestor_tiles):
    masked = mask_panels(panels, ancestor_tiles)[0]
    ys, own = products(inverse_tile, masked)
    anc, diag, cross = finish(ys, own, link_panel[0], diag_inverse[0])
    return anc[None], diag[None], cross[None]


def solution(mesh):
    in_specs = (
        P(("hyp", "row"), "col"),
        P("hyp", None, ("col", "row"), None),
        P("hyp", None, None),
        P("hyp", None, "row", "col"),
        P(),
    )
    out_specs = (
        P("hyp", None, ("row", "col"), None),
        P("hyp", None, "row", "col"),
        P("hyp", "row", "col"),
    )
    return jax.shard_map(local, mesh=mesh, in_specs=in_specs, out_specs=out_specs, check_vma=False)
```

profile of v0, /device:TPU:3, one launch (start us, length us, event | category | flops | bytes accessed | tf_op | source)
XLA Modules:
  0.0 221.5 jit_solution(2641993256261886501)
XLA Ops:
  0.6 0.0 copy-start
  0.7 0.7 copy-done
  1.3 0.1 broadcast_bitcast_fusion
  1.4 0.1 copy.10
  1.5 3.1 %select_bitcast_fusion.x_hbm = f32[2,512,512]{2,1,0:T(8,128)} fusion(f32[1,2,512,512]{3,2,1,0:T(8,128)} %param.6, pred[2,512]{1,0:T(4,128)(4,1)S(1)} %dynamic-slice_compare_fusion), kind=kLoop, calls=%fused_computation | loop fusion | flops 524288 | bytes 4195328 | tf_op jit(solution)/shard_map/squeeze | solution.py:414
  4.6 0.0 copy-start.2
  4.6 0.0 copy-start.3
  4.6 174.5 %shard_map.79 = (f32[2,512,512]{2,1,0:T(8,128)}, f32[2,512,512]{2,1,0:T(8,128)}) custom-call(f32[2048,2048]{1,0:T(8,128)} %a_hbm.1, f32[2,512,512]{2,1,0:T(8,128)} %select_bitcast_fusion.x_hbm), custom_call_target="tpu_custom_call" | custom-call | tf_op jit(solution)/shard_map/pallas_call | solution.py:255
  179.1 0.0 copy-done.2
  179.1 0.0 copy-done.3
  179.2 0.0 copy-start.1
  179.2 1.6 copy-done.1
  180.8 38.2 %shard_map.80 = (f32[2,512,512]{2,1,0:T(8,128)S(1)}, f32[2,128,128]{2,1,0:T(8,128)S(1)}, f32[128,128]{1,0:T(8,128)S(1)}) custom-call(f32[2,512,512]{2,1,0:T(8,128)S(1)} %copy-done.1, f32[2,512,512]{2,1,0:T(8,128)} %get-tuple-element.9.own_ref, f32[512,512]{1,0:T(8,128)S(1)} %bitcast.15, f32[2,128,128]{2,1,0:T(8,128)S(1)} %bitcast.17), custom_call_target="tpu_custom_call" | custom-call | tf_op jit(solution)/shard_map/pallas_call | solution.py:392
  218.9 1.3 copy.14
  220.2 0.7 copy.15
  220.9 0.6 copy.16
  (1 shorter events, 0.0 us)
Async XLA Ops:
  0.6 0.7 copy-start
  4.6 174.5 %copy-start.2 = (f32[1,512,512]{2,1,0:T(8,128)S(1)}, f32[1,512,512]{2,1,0:T(8,128)}, u32[]{:S(2)}) copy-start(f32[1,512,512]{2,1,0:T(8,128)} %param.7) | copy-start | bytes 3145732
  4.6 174.5 %copy-start.3 = (f32[1,2,128,128]{3,2,1,0:T(8,128)S(1)}, f32[1,2,128,128]{3,2,1,0:T(8,128)}, u32[]{:S(2)}) copy-start(f32[1,2,128,128]{3,2,1,0:T(8,128)} %param.8) | copy-start | bytes 393220
  179.2 1.6 copy-start.1
where the time goes:
time: 222 us
  Pallas kernels  213 us (96%)
  local copies, waits for them, and re-layouts  5 us (2%)
  other arithmetic  3.15 us (1%)
    pallas_call x1, Pallas kernels, products(): pl.pallas_call(functools.partial(exchange, (rows_axis, cols_axis), chunks...  175 us
    pallas_call x1, Pallas kernels, finish(): pl.pallas_call(functools.partial(finish_kernel, levels, count), out_shape...  38.2 us
    unnamed x13, local copies, waits for them, and re-layouts  5 us

commit v1 on v0

--- a/solution.py
+++ b/solution.py
@@ -410,10 +410,487 @@
     )(y, own, link, given)
 
 
+def order_of(r, count, i):
+    near = jnp.minimum(r, count - 1 - r)
+    close = r + ((i + 1) // 2) * (1 - 2 * (i % 2))
+    far = jnp.where(2 * r < count - 1, r + i - near, r - i + near)
+    return jnp.where(i <= 2 * near, close, far)
+
+
+def fused_kernel(axis_sizes, tiles_ref, a_hbm, x_hbm, link_hbm, given_hbm, anc_ref, diag_ref, cross_ref,
+                 a_hi, a_lo, stage, pieces, gathered, partial, pair_in, group_in, own, link, given, shift_x, shift_y,
+                 given_link, term, term_pair, term_group, term_row,
+                 stage_sem, load_sem, small_sem, hop_send, hop_recv, pair_send, pair_recv, group_send, group_recv,
+                 own_send, own_recv, tp_send, tp_recv, tg_send, tg_recv, tr_send, tr_recv):
+    rows_axis, cols_axis = axis_sizes
+    groups = cols_axis // 2
+    r = lax.axis_index("row")
+    c = lax.axis_index("col")
+    g, k = c // 2, c % 2
+    chunks, _, rows, width = gathered.shape
+    height, span = given.shape[1:]
+    tile = stage.shape[1]
+    tiles = a_hbm.shape[0] // tile
+    last = chunks - 1
+
+    def remote(src, dst, send, recv, **where):
+        return pltpu.make_async_remote_copy(src, dst, send, recv, device_id=where, device_id_type=MESH)
+
+    def load(q):
+        src = x_hbm.at[q // cols_axis, :, pl.ds(pl.multiple_of((q % cols_axis) * width, width), width)]
+        return pltpu.make_async_copy(src, gathered.at[q, r], load_sem.at[q])
+
+    def stage_copy(i):
+        src = a_hbm.at[pl.ds(pl.multiple_of(i * tile, tile), tile)]
+        return pltpu.make_async_copy(src, stage.at[i % 2], stage_sem.at[i % 2])
+
+    def hop(q, block, way, target):
+        ref = gathered.at[q, block]
+        return remote(ref, ref, hop_send.at[way, q, block], hop_recv.at[q, block], row=target)
+
+    def send_own_block(q):
+        @pl.when(r + 1 < rows_axis)
+        def _():
+            hop(q, r, 0, r + 1).start()
+
+        @pl.when(r >= 1)
+        def _():
+            hop(q, r, 1, r - 1).start()
+
+    def pair_copy(q, t):
+        return remote(partial.at[q, 2 * t + 1 - k], pair_in.at[q, t], pair_send.at[q, t], pair_recv.at[q, t],
+                      col=c + 1 - 2 * k)
+
+    def group_copy(q, shift):
+        target = 2 * ((g + shift) % groups) + k
+        return remote(partial.at[q, target], group_in.at[q, shift - 1], group_send.at[q, shift - 1],
+                      group_recv.at[q, shift - 1], col=target)
+
+    def own_copy(q, target):
+        return remote(gathered.at[q, (r * cols_axis + target) % rows_axis], own.at[q], own_send.at[q, target],
+                      own_recv.at[q], col=target)
+
+    own_root = (r * cols_axis + c) // rows_axis
+
+    def each_own(act, block=None):
+        for shift in range(1, cols_axis):
+            target = (c + shift) % cols_axis
+            place = r * cols_axis + target
+            mine = place // rows_axis == c
+            if block is not None:
+                mine = mine & (place % rows_axis == block)
+
+            @pl.when(mine)
+            def _():
+                act(target)
+
+    def own_ready(q):
+        @pl.when(own_root == c)
+        def _():
+            own[q] = gathered[q, (r * cols_axis + c) % rows_axis]
+
+        @pl.when(own_root != c)
+        def _():
+            own_copy(q, c).wait_recv()
+
+    def tp_copy(n, j):
+        return remote(term.at[n, j], term_pair.at[n, j // 2], tp_send.at[n, j], tp_recv.at[n, j],
+                      col=c + 1 - 2 * k)
+
+    def tg_copy(n, j, shift):
+        return remote(term.at[n, j], term_group.at[n, shift - 1], tg_send.at[n, j],
+                      tg_recv.at[n, shift - 1], col=j)
+
+    def tr_copy(n, target):
+        return remote(term.at[n, c, target], term_row.at[n, r], tr_send.at[n, target],
+                      tr_recv.at[n, r], row=target)
+
+    def tr_wait(n, source):
+        return remote(term.at[n, c, source], term_row.at[n, source], tr_send.at[n, source],
+                      tr_recv.at[n, source], row=source)
+
+    def term_start(n, j):
+        @pl.when(j % 2 != k)
+        def _():
+            tp_copy(n, j).start()
+
+    def term_mid(n, j):
+        @pl.when(j % 2 == k)
+        def _():
+            tp_copy(n, j).wait_recv()
+            term[n, j] += term_pair[n, j // 2]
+
+            @pl.when(j != c)
+            def _():
+                tg_copy(n, j, (j // 2 - g + groups) % groups).start()
+
+    def term_far(n, j):
+        @pl.when(j == c)
+        def _():
+            total = term[n, j]
+            for shift in range(1, groups):
+                tg_copy(n, j, shift).wait_recv()
+                total += term_group[n, shift - 1]
+            term[n, j] = total
+            for shift in range(1, rows_axis):
+                tr_copy(n, (r + shift) % rows_axis).start()
+
+    def term_end(n):
+        total = term[n, c, r]
+        for shift in range(1, rows_axis):
+            source = (r + shift) % rows_axis
+            tr_wait(n, source).wait_recv()
+            total += term_row[n, source]
+        return total
+
+    def term_drain(n, j):
+        @pl.when(j % 2 != k)
+        def _():
+            tp_copy(n, j).wait_send()
+
+        @pl.when((j % 2 == k) & (j != c))
+        def _():
+            tg_copy(n, j, (j // 2 - g + groups) % groups).wait_send()
+
+    def each_column(act, stop=cols_axis):
+        def body(j, carry):
+            act(j)
+            return carry
+
+        lax.fori_loop(0, stop, body, 0)
+
+    def wide(ref, start, stop):
+        return jnp.concatenate([ref[start + j] for j in range(stop)], axis=1)
+
+    for q in range(chunks):
+        load(q).start()
+    small = [pltpu.make_async_copy(link_hbm, link, small_sem.at[0]),
+             pltpu.make_async_copy(given_hbm, given, small_sem.at[1])]
+    stage_copy(0).start()
+    stage_copy(1).start()
+    for copy in small:
+        copy.start()
+    barrier = pltpu.get_barrier_semaphore()
+    for shift in range(1, cols_axis):
+        pl.semaphore_signal(barrier, inc=1, device_id={"col": (c + shift) % cols_axis}, device_id_type=MESH)
+    for shift in range(1, rows_axis):
+        pl.semaphore_signal(barrier, inc=1, device_id={"row": (r + shift) % rows_axis}, device_id_type=MESH)
+
+    per_block = rows // TILE
+    first_tile = (c * rows_axis + r) * per_block
+
+    def mask(q, carry):
+        load(q).wait()
+        for s in range(per_block):
+            kept = (tiles_ref[q // cols_axis, first_tile + s] != 0).astype(jnp.float32)
+            at = pl.ds(s * TILE, TILE)
+            gathered[q, r, at] = gathered[q, r, at] * kept
+        return carry
+
+    lax.fori_loop(0, 2, mask, 0)
+    pl.semaphore_wait(barrier, cols_axis + rows_axis - 2)
+    send_own_block(0)
+    send_own_block(1)
+    lax.fori_loop(2, chunks, mask, 0)
+
+    def split_tile(i, carry):
+        stage_copy(i).wait()
+        at = pl.ds(pl.multiple_of(i * tile, tile), tile)
+        value = stage[i % 2]
+        high = value.astype(jnp.bfloat16)
+        a_hi[at, :] = high
+        a_lo[at, :] = (value - high.astype(jnp.float32)).astype(jnp.bfloat16)
+
+        @pl.when(i + 2 < tiles)
+        def _():
+            stage_copy(i + 2).start()
+
+        return carry
+
+    lax.fori_loop(0, tiles, split_tile, 0)
+
+    def multiply(q, block, first):
+        value = gathered[q, block]
+        high = value.astype(jnp.bfloat16)
+        pieces[:, :width] = high
+        pieces[:, width:] = (value - high.astype(jnp.float32)).astype(jnp.bfloat16)
+        inner = pl.ds(pl.multiple_of(block * rows, rows), rows)
+
+        def body(i, carry):
+            t = (c + 1 + i) % cols_axis
+            at = pl.ds(pl.multiple_of(t * rows, rows), rows)
+            both = jnp.dot(a_hi[at, inner], pieces[...], preferred_element_type=jnp.float32)
+            out = jnp.dot(a_lo[at, inner], pieces[:, :width], preferred_element_type=jnp.float32)
+            out += both[:, width:]
+            out += both[:, :width]
+            if first:
+                partial[q, t] = out
+            else:
+                partial[q, t] += out
+            return carry
+
+        lax.fori_loop(0, cols_axis, body, 0)
+
+    def pair_start(q):
+        for t in range(groups):
+            pair_copy(q, t).start()
+
+    def pair_finish(q):
+        for t in range(groups):
+            pair_copy(q, t).wait_recv()
+        for shift in range(1, groups):
+            far = (g + shift) % groups
+            partial[q, 2 * far + k] += pair_in[q, far]
+            group_copy(q, shift).start()
+
+    def total_of(q):
+        total = partial[q, c] + pair_in[q, g]
+        for shift in range(1, groups):
+            group_copy(q, shift).wait_recv()
+            total += group_in[q, shift - 1]
+        return total
+
+    def store_terms(n, value, j):
+        for i in range(rows_axis):
+            term[n, j, i] = value[i * height : (i + 1) * height]
+
+    def first_done(_):
+        for j in range(cols_axis):
+            own_ready(j)
+        y_parts = split(-anc_ref[0])
+        x_parts = split(wide(own, 0, cols_axis))
+        value = dot3(x_parts, y_parts, 0)
+        for j in range(cols_axis):
+            store_terms(0, value[:, j * span : (j + 1) * span], j)
+        each_column(lambda j: term_start(0, j))
+        for copy in small:
+            copy.wait()
+        link_parts = split(link[...])
+        value = dot3(y_parts, link_parts, 1)
+        for j in range(cols_axis):
+            shift_y[j] = value[:, j * width : (j + 1) * width]
+        value = dot3(x_parts, link_parts, 1)
+        for j in range(cols_axis):
+            shift_x[j] = value[:, j * width : (j + 1) * width]
+        link_cols = link[pl.ds(pl.multiple_of(c * span, span), span), :]
+        value = dot3(split(given[0]), split(link_cols), 1)
+        for j in range(cols_axis):
+            given_link[j] = value[:, j * span : (j + 1) * span]
+
+    def own_shifted(j):
+        own_ready(cols_axis + j)
+        own[cols_axis + j] -= shift_x[j]
+
+    def cross_term(j):
+        value = dot3(split(anc_ref[0]), split(own[cols_axis + j]), 0)
+        store_terms(1, -value, j)
+        term[1, j, r] -= given_link[j]
+        term_start(1, j)
+
+    def second_chunk(j, total):
+        value = shift_y[j] - total
+        anc_ref[1, :, pl.ds(pl.multiple_of(j * width, width), width)] = value
+
+    def chunk(q, carry):
+        prior = q - 1
+
+        @pl.when((q >= 1) & (q < last))
+        def _():
+            send_own_block(q + 1)
+
+        each_own(lambda target: own_copy(q, target).start(), r)
+        multiply(q, r, True)
+        for i in range(1, rows_axis):
+            block = order_of(r, rows_axis, i)
+            wait_and_forward(q, block)
+            each_own(lambda target: own_copy(q, target).start(), block)
+            multiply(q, block, False)
+            if i == 1:
+                @pl.when(q >= 1)
+                def _():
+                    pair_finish(prior)
+
+                @pl.when(q == cols_axis + 1)
+                def _():
+                    each_column(lambda j: term_mid(0, j))
+
+                @pl.when(q >= cols_axis + 2)
+                def _():
+                    term_mid(1, q - cols_axis - 2)
+
+            if i == rows_axis - 1:
+                @pl.when((q >= 1) & (q <= cols_axis))
+                def _():
+                    at = pl.ds(pl.multiple_of(prior * width, width), width)
+                    anc_ref[0, :, at] = -total_of(prior)
+
+                @pl.when(q == cols_axis)
+                def _():
+                    first_done(None)
+
+                @pl.when(q == cols_axis + 1)
+                def _():
+                    each_column(lambda j: term_far(0, j))
+
+                @pl.when(q >= cols_axis + 2)
+                def _():
+                    term_far(1, q - cols_axis - 2)
+
+                @pl.when(q >= cols_axis + 1)
+                def _():
+                    j = prior - cols_axis
+                    second_chunk(j, total_of(prior))
+                    own_shifted(j)
+                    cross_term(j)
+
+        pair_start(q)
+        return carry
+
+    def wait_and_forward(q, block):
+        @pl.when(block < r)
+        def _():
+            hop(q, block, 0, r - 1).wait_recv()
+
+            @pl.when(r + 1 < rows_axis)
+            def _():
+                hop(q, block, 0, r + 1).start()
+
+        @pl.when(block > r)
+        def _():
+            hop(q, block, 1, r + 1).wait_recv()
+
+            @pl.when(r >= 1)
+            def _():
+                hop(q, block, 1, r - 1).start()
+
+    lax.fori_loop(0, chunks, chunk, 0)
+
+    end = cols_axis - 1
+    pair_finish(last)
+    own_shifted(end)
+    cross_term(end)
+    term_mid(1, end - 1)
+    link_rows = link[pl.ds(pl.multiple_of(r * height, height), height), :]
+    base = dot3(split(link_rows), split(jnp.concatenate([given_link[j] for j in range(cols_axis)], axis=1)), 0)
+    shifted = split(wide(own, cols_axis, cols_axis))
+    for j in range(cols_axis - 1):
+        value = base[:, j * span : (j + 1) * span] - dot3(
+            shifted, split(anc_ref[1, :, j * width : (j + 1) * width]), 0)
+        store_terms(2, value, j)
+        term_start(2, j)
+    term_far(1, end - 1)
+    second_chunk(end, total_of(last))
+    value = base[:, end * span :] - dot3(shifted, split(anc_ref[1, :, end * width :]), 0)
+    store_terms(2, value, end)
+    term_start(2, end)
+    each_column(lambda j: term_mid(2, j))
+    term_mid(1, end)
+    each_column(lambda j: term_far(2, j))
+    term_far(1, end)
+    diag_ref[0] = given[0] + term_end(0)
+    cross_ref[...] = term_end(1)
+    diag_ref[1] = given[1] + term_end(2)
+
+    def drain(q, carry):
+        def body(block, carry):
+            @pl.when((block <= r) & (r + 1 < rows_axis))
+            def _():
+                hop(q, block, 0, r + 1).wait_send()
+
+            @pl.when((block >= r) & (r >= 1))
+            def _():
+                hop(q, block, 1, r - 1).wait_send()
+
+            return carry
+
+        lax.fori_loop(0, rows_axis, body, 0)
+        each_own(lambda target: own_copy(q, target).wait_send())
+        for t in range(groups):
+            pair_copy(q, t).wait_send()
+        for shift in range(1, groups):
+            group_copy(q, shift).wait_send()
+        return carry
+
+    lax.fori_loop(0, chunks, drain, 0)
+    for n in range(3):
+        each_column(lambda j: term_drain(n, j))
+        for shift in range(1, rows_axis):
+            tr_copy(n, (r + shift) % rows_axis).wait_send()
+
+
+def fused(inverse_tile, panels, link_panel, given, tiles):
+    rows_axis, cols_axis = lax.axis_size("row"), lax.axis_size("col")
+    groups = cols_axis // 2
+    full, depth = inverse_tile.shape
+    count, rows, columns = panels.shape
+    height, span = given.shape[1:]
+    width = span
+    chunks = count * cols_axis
+    tile = min(128, full)
+    f32, bf16 = jnp.float32, jnp.bfloat16
+    dma = pltpu.SemaphoreType.DMA
+    vmem = pltpu.VMEM
+    return pl.pallas_call(
+        functools.partial(fused_kernel, (rows_axis, cols_axis)),
+        out_shape=(
+            jax.ShapeDtypeStruct((count, rows, columns), f32),
+            jax.ShapeDtypeStruct(given.shape, f32),
+            jax.ShapeDtypeStruct((height, span), f32),
+        ),
+        in_specs=[pl.BlockSpec(memory_space=pltpu.SMEM)] + [pl.BlockSpec(memory_space=pl.ANY)] * 4,
+        out_specs=[pl.BlockSpec(memory_space=vmem)] * 3,
+        scratch_shapes=[
+            vmem((full, depth), bf16),
+            vmem((full, depth), bf16),
+            vmem((2, tile, depth), f32),
+            vmem((rows, 2 * width), bf16),
+            vmem((chunks, rows_axis, rows, width), f32),
+            vmem((chunks, cols_axis, rows, width), f32),
+            vmem((chunks, groups, rows, width), f32),
+            vmem((chunks, max(groups - 1, 1), rows, width), f32),
+            vmem((chunks, rows, width), f32),
+            vmem((columns, columns), f32),
+            vmem(given.shape, f32),
+            vmem((cols_axis, rows, width), f32),
+            vmem((cols_axis, rows, width), f32),
+            vmem((cols_axis, height, span), f32),
+            vmem((3, cols_axis, rows_axis, height, span), f32),
+            vmem((3, groups, rows_axis, height, span), f32),
+            vmem((3, max(groups - 1, 1), rows_axis, height, span), f32),
+            vmem((3, rows_axis, height, span), f32),
+            dma((2,)),
+            dma((chunks,)),
+            dma((2,)),
+            dma((2, chunks, rows_axis)),
+            dma((chunks, rows_axis)),
+            dma((chunks, groups)),
+            dma((chunks, groups)),
+            dma((chunks, max(groups - 1, 1))),
+            dma((chunks, max(groups - 1, 1))),
+            dma((chunks, cols_axis)),
+            dma((chunks,)),
+            dma((3, cols_axis)),
+            dma((3, cols_axis)),
+            dma((3, cols_axis)),
+            dma((3, max(groups - 1, 1))),
+            dma((3, rows_axis)),
+            dma((3, rows_axis)),
+        ],
+        compiler_params=pltpu.CompilerParams(
+            collective_id=2, has_side_effects=True, vmem_limit_bytes=62 * 1024 * 1024),
+    )(tiles, inverse_tile, panels, link_panel, given)
+
+
 def local(inverse_tile, panels, link_panel, diag_inverse, ancestor_tiles):
-    masked = mask_panels(panels, ancestor_tiles)[0]
-    ys, own = products(inverse_tile, masked)
-    anc, diag, cross = finish(ys, own, link_panel[0], diag_inverse[0])
+    rows_axis, cols_axis = lax.axis_size("row"), lax.axis_size("col")
+    rows, columns = panels.shape[2:]
+    square = rows % TILE == 0 and (columns // cols_axis) % 128 == 0 and cols_axis % 2 == 0 and rows_axis > 1
+    if square:
+        anc, diag, cross = fused(inverse_tile, panels[0], link_panel[0], diag_inverse[0], ancestor_tiles[0])
+    else:
+        masked = mask_panels(panels, ancestor_tiles)[0]
+        ys, own = products(inverse_tile, masked)
+        anc, diag, cross = finish(ys, own, link_panel[0], diag_inverse[0])
     return anc[None], diag[None], cross[None]
 
 

time: 222 us -> 192 us (0.86)
  Pallas kernels: 213 us -> 186 us
  other arithmetic: 3.15 us -> 0 us
    pallas_call x2 -> x1, Pallas kernels: 213 us -> 186 us  [fused(): pl.pallas_call(functools.partial(fused_kernel, (rows_axis, cols_axis)), o...]
    squeeze x1 -> x0, other arithmetic: 3.13 us -> none  [local(): masked = mask_panels(panels, ancestor_tiles)[0]]
    unnamed x13 -> x7, local copies, waits for them, and re-layouts: 5 us -> 4.41 us
where the time goes in v1:
time: 192 us; the launch traced here: 191 us
  Pallas kernels  186 us (97%)
  local copies, waits for them, and re-layouts  4.41 us (2%)
    pallas_call x1, Pallas kernels, fused(): pl.pallas_call(functools.partial(fused_kernel, (rows_axis, cols_axis)), o...  186 us
    unnamed x7, local copies, waits for them, and re-layouts  4.41 us

profile of v1, /device:TPU:3, one launch (start us, length us, event | category | flops | bytes accessed | tf_op | source)
XLA Modules:
  0.0 191.2 jit_solution(37682985690592889)
XLA Ops:
  0.6 186.1 %shard_map.76 = (f32[2,512,512]{2,1,0:T(8,128)}, f32[2,128,128]{2,1,0:T(8,128)}, f32[128,128]{1,0:T(8,128)}) custom-call(s32[2,64]{1,0:T(2,128)} %bitcast.13, f32[2048,2048]{1,0:T(8,128)} %a_hbm.1, f32[2,512,512]{2,1,0:T(8,128)} %bitcast.7, f32[512,512]{1,0:T(8,128)} %bitcast.9, f32[2,128,128]{2,1,0:T(8,128)} %bitcast.10), custom_call_target="tpu_custom_call" | custom-call | tf_op jit(solution)/shard_map/pallas_call | solution.py:833
  186.8 0.0 copy-start
  186.8 0.0 copy-start.1
  186.8 3.1 %copy.11 = f32[1,2,512,512]{3,2,1,0:T(8,128)} copy(f32[1,2,512,512]{3,2,1,0:T(8,128)} %bitcast.8) | data formatting | bytes 4194304
  189.9 0.0 copy-done
  189.9 0.7 copy.12
  190.6 0.0 copy-done.1
  190.6 0.6 copy.13
Async XLA Ops:
  186.8 3.1 %copy-start = (f32[2,128,128]{2,1,0:T(8,128)S(1)}, f32[2,128,128]{2,1,0:T(8,128)}, u32[]{:S(2)}) copy-start(f32[2,128,128]{2,1,0:T(8,128)} %get-tuple-element.7) | copy-start | bytes 393220
  186.8 3.8 %copy-start.1 = (f32[128,128]{1,0:T(8,128)S(1)}, f32[128,128]{1,0:T(8,128)}, u32[]{:S(2)}) copy-start(f32[128,128]{1,0:T(8,128)} %get-tuple-element.8) | copy-start | bytes 196612

commit v2 on v1

--- a/solution.py
+++ b/solution.py
@@ -421,7 +421,8 @@
                  a_hi, a_lo, stage, pieces, gathered, partial, pair_in, group_in, own, link, given, shift_x, shift_y,
                  given_link, term, term_pair, term_group, term_row,
                  stage_sem, load_sem, small_sem, hop_send, hop_recv, pair_send, pair_recv, group_send, group_recv,
-                 own_send, own_recv, tp_send, tp_recv, tg_send, tg_recv, tr_send, tr_recv):
+                 own_send, own_recv, tp_send, tp_recv, tg_send, tg_recv, tr_send, tr_recv,
+                 corner, corner_pair, corner_group, corner_row, cp_sem, cg_send, cg_recv, cr_send, cr_recv):
     rows_axis, cols_axis = axis_sizes
     groups = cols_axis // 2
     r = lax.axis_index("row")
@@ -432,6 +433,7 @@
     tile = stage.shape[1]
     tiles = a_hbm.shape[0] // tile
     last = chunks - 1
+    end = cols_axis - 1
 
     def remote(src, dst, send, recv, **where):
         return pltpu.make_async_remote_copy(src, dst, send, recv, device_id=where, device_id_type=MESH)
@@ -449,13 +451,66 @@
         return remote(ref, ref, hop_send.at[way, q, block], hop_recv.at[q, block], row=target)
 
     def send_own_block(q):
-        @pl.when(r + 1 < rows_axis)
+        @pl.when((r + 1 < rows_axis) & ((q < last) | (r >= c)))
         def _():
             hop(q, r, 0, r + 1).start()
 
-        @pl.when(r >= 1)
+        @pl.when((r >= 1) & ((q < last) | (r <= c)))
         def _():
             hop(q, r, 1, r - 1).start()
+
+    def send_early():
+        @pl.when(r < c)
+        def _():
+            hop(last, r, 0, r + 1).start()
+
+        @pl.when(r > c)
+        def _():
+            hop(last, r, 1, r - 1).start()
+
+    def pass_early(distance):
+        @pl.when((r - distance >= 0) & (r <= c))
+        def _():
+            block = r - distance
+            hop(last, block, 0, r - 1).wait_recv()
+
+            @pl.when(r < c)
+            def _():
+                hop(last, block, 0, r + 1).start()
+
+            @pl.when(r == c)
+            def _():
+                own_copy(last, block).start()
+
+        @pl.when((r + distance < rows_axis) & (r >= c))
+        def _():
+            block = r + distance
+            hop(last, block, 1, r + 1).wait_recv()
+
+            @pl.when(r > c)
+            def _():
+                hop(last, block, 1, r - 1).start()
+
+            @pl.when(r == c)
+            def _():
+                own_copy(last, block).start()
+
+    def wait_and_forward(q, block):
+        @pl.when((block < r) & ((q < last) | (r > c)))
+        def _():
+            hop(q, block, 0, r - 1).wait_recv()
+
+        @pl.when((block > r) & ((q < last) | (r < c)))
+        def _():
+            hop(q, block, 1, r + 1).wait_recv()
+
+        @pl.when((block < r) & (r + 1 < rows_axis) & ((q < last) | (r >= c)))
+        def _():
+            hop(q, block, 0, r + 1).start()
+
+        @pl.when((block > r) & (r >= 1) & ((q < last) | (r <= c)))
+        def _():
+            hop(q, block, 1, r - 1).start()
 
     def pair_copy(q, t):
         return remote(partial.at[q, 2 * t + 1 - k], pair_in.at[q, t], pair_send.at[q, t], pair_recv.at[q, t],
@@ -467,29 +522,14 @@
                       group_recv.at[q, shift - 1], col=target)
 
     def own_copy(q, target):
-        return remote(gathered.at[q, (r * cols_axis + target) % rows_axis], own.at[q], own_send.at[q, target],
-                      own_recv.at[q], col=target)
-
-    own_root = (r * cols_axis + c) // rows_axis
-
-    def each_own(act, block=None):
-        for shift in range(1, cols_axis):
-            target = (c + shift) % cols_axis
-            place = r * cols_axis + target
-            mine = place // rows_axis == c
-            if block is not None:
-                mine = mine & (place % rows_axis == block)
-
-            @pl.when(mine)
-            def _():
-                act(target)
+        return remote(gathered.at[q, target], own.at[q], own_send.at[q, target], own_recv.at[q], col=target)
 
     def own_ready(q):
-        @pl.when(own_root == c)
-        def _():
-            own[q] = gathered[q, (r * cols_axis + c) % rows_axis]
-
-        @pl.when(own_root != c)
+        @pl.when(r == c)
+        def _():
+            own[q] = gathered[q, c]
+
+        @pl.when(r != c)
         def _():
             own_copy(q, c).wait_recv()
 
@@ -532,8 +572,10 @@
                 tg_copy(n, j, shift).wait_recv()
                 total += term_group[n, shift - 1]
             term[n, j] = total
-            for shift in range(1, rows_axis):
-                tr_copy(n, (r + shift) % rows_axis).start()
+
+    def term_rows(n):
+        for shift in range(1, rows_axis):
+            tr_copy(n, (r + shift) % rows_axis).start()
 
     def term_end(n):
         total = term[n, c, r]
@@ -609,7 +651,7 @@
 
     lax.fori_loop(0, tiles, split_tile, 0)
 
-    def multiply(q, block, first):
+    def multiply(q, block, first, final=False):
         value = gathered[q, block]
         high = value.astype(jnp.bfloat16)
         pieces[:, :width] = high
@@ -617,7 +659,8 @@
         inner = pl.ds(pl.multiple_of(block * rows, rows), rows)
 
         def body(i, carry):
-            t = (c + 1 + i) % cols_axis
+            near = (g + 1 + i) % groups
+            t = 2 * near + jnp.where(i < groups, 1 - k, k)
             at = pl.ds(pl.multiple_of(t * rows, rows), rows)
             both = jnp.dot(a_hi[at, inner], pieces[...], preferred_element_type=jnp.float32)
             out = jnp.dot(a_lo[at, inner], pieces[:, :width], preferred_element_type=jnp.float32)
@@ -627,13 +670,14 @@
                 partial[q, t] = out
             else:
                 partial[q, t] += out
+            if final:
+                @pl.when(i < groups)
+                def _():
+                    pair_copy(q, near).start()
+
             return carry
 
         lax.fori_loop(0, cols_axis, body, 0)
-
-    def pair_start(q):
-        for t in range(groups):
-            pair_copy(q, t).start()
 
     def pair_finish(q):
         for t in range(groups):
@@ -691,24 +735,67 @@
         value = shift_y[j] - total
         anc_ref[1, :, pl.ds(pl.multiple_of(j * width, width), width)] = value
 
+    def second_terms():
+        shifted = split(wide(own, cols_axis, cols_axis))
+        done = split(anc_ref[1, :, : end * width])
+        link_rows = link[pl.ds(pl.multiple_of(r * height, height), height), :]
+        base = dot3(split(link_rows), split(wide(given_link, 0, cols_axis)), 0)
+        value = dot3(shifted, done, 0)
+        for j in range(end):
+            at = slice(j * span, (j + 1) * span)
+            store_terms(2, base[:, at] - value[:, at], j)
+        value = dot3(done, split(own[last]), 0)
+        for i in range(end):
+            at = slice(i * height, (i + 1) * height)
+            term[2, end, i] = base[at, end * span :] - value[at]
+        term[2, end, end] = base[end * height :, end * span :]
+        each_column(lambda j: term_start(2, j))
+
     def chunk(q, carry):
         prior = q - 1
 
-        @pl.when((q >= 1) & (q < last))
-        def _():
-            send_own_block(q + 1)
-
-        each_own(lambda target: own_copy(q, target).start(), r)
+        @pl.when(q + 2 <= last)
+        def _():
+            send_own_block(q + 2)
+
+        @pl.when(q == end - 1)
+        def _():
+            send_early()
+
         multiply(q, r, True)
+
+        @pl.when(q >= 1)
+        def _():
+            pair_finish(prior)
+
         for i in range(1, rows_axis):
             block = order_of(r, rows_axis, i)
+            if i == rows_axis - 1:
+                @pl.when(q == cols_axis + 1)
+                def _():
+                    each_column(lambda j: term_far(0, j))
+
+                @pl.when(q >= cols_axis + 2)
+                def _():
+                    term_far(1, q - cols_axis - 2)
+
+                @pl.when(q == last)
+                def _():
+                    term_far(1, end)
+                    term_mid(1, end - 1)
+                    each_column(lambda j: term_mid(2, j))
+
             wait_and_forward(q, block)
-            each_own(lambda target: own_copy(q, target).start(), block)
-            multiply(q, block, False)
+
+            @pl.when((r == c) & (q < last))
+            def _():
+                own_copy(q, block).start()
+
+            multiply(q, block, False, i == rows_axis - 1)
             if i == 1:
-                @pl.when(q >= 1)
-                def _():
-                    pair_finish(prior)
+                @pl.when((q >= end) & (q < end + rows_axis - 1))
+                def _():
+                    pass_early(q - end + 1)
 
                 @pl.when(q == cols_axis + 1)
                 def _():
@@ -718,7 +805,11 @@
                 def _():
                     term_mid(1, q - cols_axis - 2)
 
-            if i == rows_axis - 1:
+                @pl.when(q == last)
+                def _():
+                    term_mid(1, end)
+
+            if i == 2:
                 @pl.when((q >= 1) & (q <= cols_axis))
                 def _():
                     at = pl.ds(pl.multiple_of(prior * width, width), width)
@@ -727,14 +818,6 @@
                 @pl.when(q == cols_axis)
                 def _():
                     first_done(None)
-
-                @pl.when(q == cols_axis + 1)
-                def _():
-                    each_column(lambda j: term_far(0, j))
-
-                @pl.when(q >= cols_axis + 2)
-                def _():
-                    term_far(1, q - cols_axis - 2)
 
                 @pl.when(q >= cols_axis + 1)
                 def _():
@@ -743,53 +826,94 @@
                     own_shifted(j)
                     cross_term(j)
 
-        pair_start(q)
+                @pl.when(q == last - 1)
+                def _():
+                    own_shifted(end)
+                    cross_term(end)
+
+                @pl.when(q == last)
+                def _():
+                    second_terms()
+
         return carry
 
-    def wait_and_forward(q, block):
-        @pl.when(block < r)
-        def _():
-            hop(q, block, 0, r - 1).wait_recv()
-
-            @pl.when(r + 1 < rows_axis)
-            def _():
-                hop(q, block, 0, r + 1).start()
-
-        @pl.when(block > r)
-        def _():
-            hop(q, block, 1, r + 1).wait_recv()
-
-            @pl.when(r >= 1)
-            def _():
-                hop(q, block, 1, r - 1).start()
-
     lax.fori_loop(0, chunks, chunk, 0)
 
-    end = cols_axis - 1
+    term_rows(0)
+
+    @pl.when(c != end - 1)
+    def _():
+        term_rows(1)
+
     pair_finish(last)
-    own_shifted(end)
-    cross_term(end)
-    term_mid(1, end - 1)
-    link_rows = link[pl.ds(pl.multiple_of(r * height, height), height), :]
-    base = dot3(split(link_rows), split(jnp.concatenate([given_link[j] for j in range(cols_axis)], axis=1)), 0)
-    shifted = split(wide(own, cols_axis, cols_axis))
-    for j in range(cols_axis - 1):
-        value = base[:, j * span : (j + 1) * span] - dot3(
-            shifted, split(anc_ref[1, :, j * width : (j + 1) * width]), 0)
-        store_terms(2, value, j)
-        term_start(2, j)
     term_far(1, end - 1)
+
+    @pl.when(c == end - 1)
+    def _():
+        term_rows(1)
+
+    each_column(lambda j: term_far(2, j))
+    term_rows(2)
     second_chunk(end, total_of(last))
-    value = base[:, end * span :] - dot3(shifted, split(anc_ref[1, :, end * width :]), 0)
-    store_terms(2, value, end)
-    term_start(2, end)
-    each_column(lambda j: term_mid(2, j))
-    term_mid(1, end)
-    each_column(lambda j: term_far(2, j))
-    term_far(1, end)
+    corner[...] = -dot3(split(own[last]), split(anc_ref[1, :, end * width :]), 0)
+    side, odd = end // 2, end % 2
+    to_pair = remote(corner, corner_pair, cp_sem.at[0], cp_sem.at[1], col=c + 1 - 2 * k)
+
+    def to_group(shift):
+        return remote(corner, corner_group.at[shift - 1], cg_send, cg_recv.at[shift - 1], col=end)
+
+    def to_row(source):
+        return remote(corner, corner_row.at[source], cr_send, cr_recv.at[source], row=end)
+
+    @pl.when(k != odd)
+    def _():
+        to_pair.start()
+
     diag_ref[0] = given[0] + term_end(0)
     cross_ref[...] = term_end(1)
+
+    @pl.when(k == odd)
+    def _():
+        to_pair.wait_recv()
+        corner[...] += corner_pair[...]
+
+        @pl.when(g != side)
+        def _():
+            to_group((side - g + groups) % groups).start()
+
     diag_ref[1] = given[1] + term_end(2)
+
+    @pl.when(c == end)
+    def _():
+        total = corner[...]
+        for shift in range(1, groups):
+            to_group(shift).wait_recv()
+            total += corner_group[shift - 1]
+        corner[...] = total
+
+        @pl.when(r != end)
+        def _():
+            to_row(r).start()
+
+        @pl.when(r == end)
+        def _():
+            total = diag_ref[1] + corner[...]
+            for source in range(end):
+                to_row(source).wait_recv()
+                total += corner_row[source]
+            diag_ref[1] = total
+
+    @pl.when(k != odd)
+    def _():
+        to_pair.wait_send()
+
+    @pl.when((k == odd) & (g != side))
+    def _():
+        to_group((side - g + groups) % groups).wait_send()
+
+    @pl.when((c == end) & (r != end))
+    def _():
+        to_row(r).wait_send()
 
     def drain(q, carry):
         def body(block, carry):
@@ -804,7 +928,11 @@
             return carry
 
         lax.fori_loop(0, rows_axis, body, 0)
-        each_own(lambda target: own_copy(q, target).wait_send())
+        for shift in range(1, cols_axis):
+            @pl.when(r == c)
+            def _():
+                own_copy(q, (c + shift) % cols_axis).wait_send()
+
         for t in range(groups):
             pair_copy(q, t).wait_send()
         for shift in range(1, groups):
@@ -875,16 +1003,25 @@
             dma((3, max(groups - 1, 1))),
             dma((3, rows_axis)),
             dma((3, rows_axis)),
+            vmem((height, span), f32),
+            vmem((height, span), f32),
+            vmem((max(groups - 1, 1), height, span), f32),
+            vmem((rows_axis, height, span), f32),
+            dma((2,)),
+            dma,
+            dma((max(groups - 1, 1),)),
+            dma,
+            dma((rows_axis,)),
         ],
         compiler_params=pltpu.CompilerParams(
-            collective_id=2, has_side_effects=True, vmem_limit_bytes=62 * 1024 * 1024),
+            collective_id=2, has_side_effects=True, vmem_limit_bytes=58 * 1024 * 1024),
     )(tiles, inverse_tile, panels, link_panel, given)
 
 
 def local(inverse_tile, panels, link_panel, diag_inverse, ancestor_tiles):
     rows_axis, cols_axis = lax.axis_size("row"), lax.axis_size("col")
     rows, columns = panels.shape[2:]
-    square = rows % TILE == 0 and (columns // cols_axis) % 128 == 0 and cols_axis % 2 == 0 and rows_axis > 1
+    square = rows_axis == cols_axis >= 4 and cols_axis % 2 == 0 and rows % TILE == 0 and (columns // cols_axis) % 128 == 0
     if square:
         anc, diag, cross = fused(inverse_tile, panels[0], link_panel[0], diag_inverse[0], ancestor_tiles[0])
     else:

time: 192 us -> 198 us (1.031)
  Pallas kernels: 186 us -> 192 us
    pallas_call x1, Pallas kernels: 186 us -> 192 us  [fused(): pl.pallas_call(functools.partial(fused_kernel, (rows_axis, cols_axis)), o...]
where the time goes in v2:
time: 198 us; the launch traced here: 197 us
  Pallas kernels  192 us (97%)
  local copies, waits for them, and re-layouts  4.41 us (2%)
    pallas_call x1, Pallas kernels, fused(): pl.pallas_call(functools.partial(fused_kernel, (rows_axis, cols_axis)), o...  192 us
    unnamed x7, local copies, waits for them, and re-layouts  4.41 us

profile of v2, /device:TPU:3, one launch (start us, length us, event | category | flops | bytes accessed | tf_op | source)
XLA Modules:
  0.0 197.2 jit_solution(2505398587769467944)
XLA Ops:
  0.6 192.1 %shard_map.76 = (f32[2,512,512]{2,1,0:T(8,128)}, f32[2,128,128]{2,1,0:T(8,128)}, f32[128,128]{1,0:T(8,128)}) custom-call(s32[2,64]{1,0:T(2,128)} %bitcast.13, f32[2048,2048]{1,0:T(8,128)} %a_hbm.1, f32[2,512,512]{2,1,0:T(8,128)} %bitcast.7, f32[512,512]{1,0:T(8,128)} %bitcast.9, f32[2,128,128]{2,1,0:T(8,128)} %bitcast.10), custom_call_target="tpu_custom_call" | custom-call | tf_op jit(solution)/shard_map/pallas_call | solution.py:961
  192.8 0.0 copy-start
  192.8 0.0 copy-start.1
  192.8 3.1 %copy.11 = f32[1,2,512,512]{3,2,1,0:T(8,128)} copy(f32[1,2,512,512]{3,2,1,0:T(8,128)} %bitcast.8) | data formatting | bytes 4194304
  195.9 0.0 copy-done
  195.9 0.7 copy.12
  196.6 0.0 copy-done.1
  196.6 0.6 copy.13
Async XLA Ops:
  192.8 3.1 %copy-start = (f32[2,128,128]{2,1,0:T(8,128)S(1)}, f32[2,128,128]{2,1,0:T(8,128)}, u32[]{:S(2)}) copy-start(f32[2,128,128]{2,1,0:T(8,128)} %get-tuple-element.7) | copy-start | bytes 393220
  192.8 3.8 %copy-start.1 = (f32[128,128]{1,0:T(8,128)S(1)}, f32[128,128]{1,0:T(8,128)}, u32[]{:S(2)}) copy-start(f32[128,128]{1,0:T(8,128)} %get-tuple-element.8) | copy-start | bytes 196612

commit v3 on v2

--- a/solution.py
+++ b/solution.py
@@ -422,7 +422,9 @@
                  given_link, term, term_pair, term_group, term_row,
                  stage_sem, load_sem, small_sem, hop_send, hop_recv, pair_send, pair_recv, group_send, group_recv,
                  own_send, own_recv, tp_send, tp_recv, tg_send, tg_recv, tr_send, tr_recv,
-                 corner, corner_pair, corner_group, corner_row, cp_sem, cg_send, cg_recv, cr_send, cr_recv):
+                 chain_in, chain_send, chain_recv,
+                 late, late_pair, late_group, late_row, lp_sem, lg_send, lg_recv, lr_send, lr_recv,
+                 bottom, bottom_pair, bottom_group, bottom_row, bp_send, bp_recv, bg_send, bg_recv, br_send, br_recv):
     rows_axis, cols_axis = axis_sizes
     groups = cols_axis // 2
     r = lax.axis_index("row")
@@ -451,74 +453,38 @@
         return remote(ref, ref, hop_send.at[way, q, block], hop_recv.at[q, block], row=target)
 
     def send_own_block(q):
-        @pl.when((r + 1 < rows_axis) & ((q < last) | (r >= c)))
+        @pl.when((r + 1 < rows_axis))
         def _():
             hop(q, r, 0, r + 1).start()
 
-        @pl.when((r >= 1) & ((q < last) | (r <= c)))
+        @pl.when((r >= 1))
         def _():
             hop(q, r, 1, r - 1).start()
 
-    def send_early():
-        @pl.when(r < c)
-        def _():
-            hop(last, r, 0, r + 1).start()
-
-        @pl.when(r > c)
-        def _():
-            hop(last, r, 1, r - 1).start()
-
-    def pass_early(distance):
-        @pl.when((r - distance >= 0) & (r <= c))
-        def _():
-            block = r - distance
-            hop(last, block, 0, r - 1).wait_recv()
-
-            @pl.when(r < c)
-            def _():
-                hop(last, block, 0, r + 1).start()
-
-            @pl.when(r == c)
-            def _():
-                own_copy(last, block).start()
-
-        @pl.when((r + distance < rows_axis) & (r >= c))
-        def _():
-            block = r + distance
-            hop(last, block, 1, r + 1).wait_recv()
-
-            @pl.when(r > c)
-            def _():
-                hop(last, block, 1, r - 1).start()
-
-            @pl.when(r == c)
-            def _():
-                own_copy(last, block).start()
-
     def wait_and_forward(q, block):
-        @pl.when((block < r) & ((q < last) | (r > c)))
+        @pl.when((block < r))
         def _():
             hop(q, block, 0, r - 1).wait_recv()
 
-        @pl.when((block > r) & ((q < last) | (r < c)))
+        @pl.when((block > r))
         def _():
             hop(q, block, 1, r + 1).wait_recv()
 
-        @pl.when((block < r) & (r + 1 < rows_axis) & ((q < last) | (r >= c)))
+        @pl.when((block < r) & (r + 1 < rows_axis))
         def _():
             hop(q, block, 0, r + 1).start()
 
-        @pl.when((block > r) & (r >= 1) & ((q < last) | (r <= c)))
+        @pl.when((block > r) & (r >= 1))
         def _():
             hop(q, block, 1, r - 1).start()
 
     def pair_copy(q, t):
-        return remote(partial.at[q, 2 * t + 1 - k], pair_in.at[q, t], pair_send.at[q, t], pair_recv.at[q, t],
+        return remote(partial.at[q % 2, 2 * t + 1 - k], pair_in.at[q, t], pair_send.at[q, t], pair_recv.at[q, t],
                       col=c + 1 - 2 * k)
 
     def group_copy(q, shift):
         target = 2 * ((g + shift) % groups) + k
-        return remote(partial.at[q, target], group_in.at[q, shift - 1], group_send.at[q, shift - 1],
+        return remote(partial.at[q % 2, target], group_in.at[q, shift - 1], group_send.at[q, shift - 1],
                       group_recv.at[q, shift - 1], col=target)
 
     def own_copy(q, target):
@@ -533,12 +499,15 @@
         def _():
             own_copy(q, c).wait_recv()
 
+    def part(n):
+        return pl.ds(0, end if n == 2 else rows_axis)
+
     def tp_copy(n, j):
-        return remote(term.at[n, j], term_pair.at[n, j // 2], tp_send.at[n, j], tp_recv.at[n, j],
+        return remote(term.at[n, j, part(n)], term_pair.at[n, j // 2, part(n)], tp_send.at[n, j], tp_recv.at[n, j],
                       col=c + 1 - 2 * k)
 
     def tg_copy(n, j, shift):
-        return remote(term.at[n, j], term_group.at[n, shift - 1], tg_send.at[n, j],
+        return remote(term.at[n, j, part(n)], term_group.at[n, shift - 1, part(n)], tg_send.at[n, j],
                       tg_recv.at[n, shift - 1], col=j)
 
     def tr_copy(n, target):
@@ -573,9 +542,19 @@
                 total += term_group[n, shift - 1]
             term[n, j] = total
 
+    def each_row(n, act):
+        for shift in range(1, rows_axis):
+            target = (r + shift) % rows_axis
+            wanted = c < end
+            if n == 2:
+                wanted = wanted & (target < end)
+
+            @pl.when(wanted)
+            def _():
+                act(target)
+
     def term_rows(n):
-        for shift in range(1, rows_axis):
-            tr_copy(n, (r + shift) % rows_axis).start()
+        each_row(n, lambda target: tr_copy(n, target).start())
 
     def term_end(n):
         total = term[n, c, r]
@@ -584,6 +563,132 @@
             tr_wait(n, source).wait_recv()
             total += term_row[n, source]
         return total
+
+    def chain_copy(way, target):
+        return remote(term.at[0, c, target], chain_in.at[way, target], chain_send.at[way, target],
+                      chain_recv.at[way, target], row=r + 1 - 2 * way)
+
+    def chain(step):
+        for way in range(2):
+            at = step if way == 0 else rows_axis - 1 - step
+            ahead = range(at + 1, rows_axis) if way == 0 else range(at)
+
+            @pl.when(r == at)
+            def _():
+                if step > 0:
+                    for target in [at, *ahead]:
+                        chain_copy(way, target).wait_recv()
+                        term[0, c, target] += chain_in[way, target]
+                for target in ahead:
+                    chain_copy(way, target).start()
+
+    def chain_drain():
+        for way in range(2):
+            for target in range(rows_axis):
+                @pl.when((target > r) if way == 0 else (target < r))
+                def _():
+                    chain_copy(way, target).wait_send()
+
+    side, odd = end // 2, end % 2
+
+    def lp_copy():
+        return remote(late, late_pair, lp_sem.at[0], lp_sem.at[1], col=c + 1 - 2 * k)
+
+    def lg_copy(shift):
+        return remote(late, late_group.at[shift - 1], lg_send, lg_recv.at[shift - 1], col=end)
+
+    def lr_copy(target, source):
+        return remote(late.at[target], late_row.at[source], lr_send.at[target], lr_recv.at[source], row=target)
+
+    def late_start():
+        @pl.when(k != odd)
+        def _():
+            lp_copy().start()
+
+    def late_mid():
+        @pl.when(k == odd)
+        def _():
+            lp_copy().wait_recv()
+            late[...] += late_pair[...]
+
+            @pl.when(g != side)
+            def _():
+                lg_copy((side - g + groups) % groups).start()
+
+    def late_far():
+        @pl.when(c == end)
+        def _():
+            total = late[...]
+            for shift in range(1, groups):
+                lg_copy(shift).wait_recv()
+                total += late_group[shift - 1]
+            late[...] = total
+            for shift in range(1, rows_axis):
+                lr_copy((r + shift) % rows_axis, r).start()
+
+    def late_drain():
+        @pl.when(k != odd)
+        def _():
+            lp_copy().wait_send()
+
+        @pl.when((k == odd) & (g != side))
+        def _():
+            lg_copy((side - g + groups) % groups).wait_send()
+
+        @pl.when(c == end)
+        def _():
+            for shift in range(1, rows_axis):
+                lr_copy((r + shift) % rows_axis, r).wait_send()
+
+    def bp_copy(j):
+        return remote(bottom.at[j], bottom_pair.at[j // 2], bp_send.at[j], bp_recv.at[j], col=c + 1 - 2 * k)
+
+    def bg_copy(j, shift):
+        return remote(bottom.at[j], bottom_group.at[shift - 1], bg_send.at[j], bg_recv.at[shift - 1], col=j)
+
+    def br_copy(source):
+        return remote(bottom.at[c], bottom_row.at[source], br_send, br_recv.at[source], row=end)
+
+    def bottom_start(j):
+        @pl.when(j % 2 != k)
+        def _():
+            bp_copy(j).start()
+
+    def bottom_mid(j):
+        @pl.when(j % 2 == k)
+        def _():
+            bp_copy(j).wait_recv()
+            bottom[j] += bottom_pair[j // 2]
+
+            @pl.when(j != c)
+            def _():
+                bg_copy(j, (j // 2 - g + groups) % groups).start()
+
+    def bottom_far(j):
+        @pl.when(j == c)
+        def _():
+            total = bottom[j]
+            for shift in range(1, groups):
+                bg_copy(j, shift).wait_recv()
+                total += bottom_group[shift - 1]
+            bottom[j] = total
+
+            @pl.when(r != end)
+            def _():
+                br_copy(r).start()
+
+    def bottom_drain(j):
+        @pl.when(j % 2 != k)
+        def _():
+            bp_copy(j).wait_send()
+
+        @pl.when((j % 2 == k) & (j != c))
+        def _():
+            bg_copy(j, (j // 2 - g + groups) % groups).wait_send()
+
+        @pl.when((j == c) & (r != end))
+        def _():
+            br_copy(r).wait_send()
 
     def term_drain(n, j):
         @pl.when(j % 2 != k)
@@ -667,9 +772,9 @@
             out += both[:, width:]
             out += both[:, :width]
             if first:
-                partial[q, t] = out
+                partial[q % 2, t] = out
             else:
-                partial[q, t] += out
+                partial[q % 2, t] += out
             if final:
                 @pl.when(i < groups)
                 def _():
@@ -684,11 +789,17 @@
             pair_copy(q, t).wait_recv()
         for shift in range(1, groups):
             far = (g + shift) % groups
-            partial[q, 2 * far + k] += pair_in[q, far]
+            partial[q % 2, 2 * far + k] += pair_in[q, far]
             group_copy(q, shift).start()
 
+    def sums_sent(q):
+        for t in range(groups):
+            pair_copy(q, t).wait_send()
+        for shift in range(1, groups):
+            group_copy(q, shift).wait_send()
+
     def total_of(q):
-        total = partial[q, c] + pair_in[q, g]
+        total = partial[q % 2, c] + pair_in[q, g]
         for shift in range(1, groups):
             group_copy(q, shift).wait_recv()
             total += group_in[q, shift - 1]
@@ -720,6 +831,7 @@
         value = dot3(split(given[0]), split(link_cols), 1)
         for j in range(cols_axis):
             given_link[j] = value[:, j * span : (j + 1) * span]
+        link_terms()
 
     def own_shifted(j):
         own_ready(cols_axis + j)
@@ -735,21 +847,39 @@
         value = shift_y[j] - total
         anc_ref[1, :, pl.ds(pl.multiple_of(j * width, width), width)] = value
 
+    def link_terms():
+        link_rows = link[pl.ds(pl.multiple_of(r * height, height), height), :]
+        value = dot3(split(link_rows), split(wide(given_link, 0, cols_axis)), 0)
+        for j in range(end):
+            store_terms(2, value[:, j * span : (j + 1) * span], j)
+        for i in range(end):
+            late[i, 1] = value[i * height : (i + 1) * height, end * span :]
+        late[end, 1] = jnp.zeros((height, span), jnp.float32)
+        for j in range(cols_axis):
+            bottom[j] = value[end * height :, j * span : (j + 1) * span]
+
     def second_terms():
-        shifted = split(wide(own, cols_axis, cols_axis))
+        value = dot3(split(wide(own, cols_axis, end)), split(anc_ref[1, :, : end * width]), 0)
+        for j in range(end):
+            for i in range(end):
+                term[2, j, i] -= value[i * height : (i + 1) * height, j * span : (j + 1) * span]
+        each_column(lambda j: term_start(2, j), end)
+
+    def late_terms():
+        shifted = split(own[last])
+        value = dot3(split(anc_ref[0]), shifted, 0)
+        for i in range(rows_axis):
+            late[i, 0] = -value[i * height : (i + 1) * height]
+        late[r, 0] -= given_link[end]
         done = split(anc_ref[1, :, : end * width])
-        link_rows = link[pl.ds(pl.multiple_of(r * height, height), height), :]
-        base = dot3(split(link_rows), split(wide(given_link, 0, cols_axis)), 0)
+        value = dot3(done, shifted, 0)
+        for i in range(end):
+            late[i, 1] -= value[i * height : (i + 1) * height]
+        late_start()
         value = dot3(shifted, done, 0)
         for j in range(end):
-            at = slice(j * span, (j + 1) * span)
-            store_terms(2, base[:, at] - value[:, at], j)
-        value = dot3(done, split(own[last]), 0)
-        for i in range(end):
-            at = slice(i * height, (i + 1) * height)
-            term[2, end, i] = base[at, end * span :] - value[at]
-        term[2, end, end] = base[end * height :, end * span :]
-        each_column(lambda j: term_start(2, j))
+            bottom[j] -= value[:, j * span : (j + 1) * span]
+            bottom_start(j)
 
     def chunk(q, carry):
         prior = q - 1
@@ -758,9 +888,9 @@
         def _():
             send_own_block(q + 2)
 
-        @pl.when(q == end - 1)
-        def _():
-            send_early()
+        @pl.when(q >= 2)
+        def _():
+            sums_sent(q - 2)
 
         multiply(q, r, True)
 
@@ -779,24 +909,19 @@
                 def _():
                     term_far(1, q - cols_axis - 2)
 
+            if i == rows_axis - 1:
                 @pl.when(q == last)
                 def _():
-                    term_far(1, end)
                     term_mid(1, end - 1)
-                    each_column(lambda j: term_mid(2, j))
 
             wait_and_forward(q, block)
 
-            @pl.when((r == c) & (q < last))
+            @pl.when(r == c)
             def _():
                 own_copy(q, block).start()
 
             multiply(q, block, False, i == rows_axis - 1)
             if i == 1:
-                @pl.when((q >= end) & (q < end + rows_axis - 1))
-                def _():
-                    pass_early(q - end + 1)
-
                 @pl.when(q == cols_axis + 1)
                 def _():
                     each_column(lambda j: term_mid(0, j))
@@ -805,9 +930,11 @@
                 def _():
                     term_mid(1, q - cols_axis - 2)
 
-                @pl.when(q == last)
-                def _():
-                    term_mid(1, end)
+            if i == rows_axis - 1:
+                for step in range(rows_axis - 1):
+                    @pl.when(q == cols_axis + 1 + step)
+                    def _():
+                        chain(step)
 
             if i == 2:
                 @pl.when((q >= 1) & (q <= cols_axis))
@@ -826,11 +953,6 @@
                     own_shifted(j)
                     cross_term(j)
 
-                @pl.when(q == last - 1)
-                def _():
-                    own_shifted(end)
-                    cross_term(end)
-
                 @pl.when(q == last)
                 def _():
                     second_terms()
@@ -839,81 +961,64 @@
 
     lax.fori_loop(0, chunks, chunk, 0)
 
-    term_rows(0)
-
     @pl.when(c != end - 1)
     def _():
         term_rows(1)
 
+    own_shifted(end)
+    late_terms()
     pair_finish(last)
+    each_column(lambda j: term_mid(2, j), end)
     term_far(1, end - 1)
 
     @pl.when(c == end - 1)
     def _():
         term_rows(1)
 
-    each_column(lambda j: term_far(2, j))
+    late_mid()
+    each_column(bottom_mid, end)
+    each_column(lambda j: term_far(2, j), end)
     term_rows(2)
     second_chunk(end, total_of(last))
-    corner[...] = -dot3(split(own[last]), split(anc_ref[1, :, end * width :]), 0)
-    side, odd = end // 2, end % 2
-    to_pair = remote(corner, corner_pair, cp_sem.at[0], cp_sem.at[1], col=c + 1 - 2 * k)
-
-    def to_group(shift):
-        return remote(corner, corner_group.at[shift - 1], cg_send, cg_recv.at[shift - 1], col=end)
-
-    def to_row(source):
-        return remote(corner, corner_row.at[source], cr_send, cr_recv.at[source], row=end)
-
-    @pl.when(k != odd)
+    bottom[end] -= dot3(split(own[last]), split(anc_ref[1, :, end * width :]), 0)
+    bottom_start(end)
+    late_far()
+    each_column(bottom_far, end)
+    chain(rows_axis - 1)
+    diag_ref[0] = given[0] + term[0, c, r]
+    bottom_mid(end)
+    bottom_far(end)
+
+    @pl.when(c < end)
     def _():
-        to_pair.start()
-
-    diag_ref[0] = given[0] + term_end(0)
-    cross_ref[...] = term_end(1)
-
-    @pl.when(k == odd)
+        cross_ref[...] = term_end(1)
+
+    @pl.when((c < end) & (r < end))
     def _():
-        to_pair.wait_recv()
-        corner[...] += corner_pair[...]
-
-        @pl.when(g != side)
-        def _():
-            to_group((side - g + groups) % groups).start()
-
-    diag_ref[1] = given[1] + term_end(2)
+        total = term[2, c, r]
+        for shift in range(1, rows_axis):
+            source = (r + shift) % rows_axis
+            tr_wait(2, source).wait_recv()
+            total += term_row[2, source]
+        diag_ref[1] = given[1] + total
 
     @pl.when(c == end)
     def _():
-        total = corner[...]
-        for shift in range(1, groups):
-            to_group(shift).wait_recv()
-            total += corner_group[shift - 1]
-        corner[...] = total
-
-        @pl.when(r != end)
-        def _():
-            to_row(r).start()
-
-        @pl.when(r == end)
-        def _():
-            total = diag_ref[1] + corner[...]
-            for source in range(end):
-                to_row(source).wait_recv()
-                total += corner_row[source]
-            diag_ref[1] = total
-
-    @pl.when(k != odd)
+        total = late[r]
+        for shift in range(1, rows_axis):
+            source = (r + shift) % rows_axis
+            lr_copy(source, source).wait_recv()
+            total += late_row[source]
+        cross_ref[...] = total[0]
+        diag_ref[1] = given[1] + total[1]
+
+    @pl.when(r == end)
     def _():
-        to_pair.wait_send()
-
-    @pl.when((k == odd) & (g != side))
-    def _():
-        to_group((side - g + groups) % groups).wait_send()
-
-    @pl.when((c == end) & (r != end))
-    def _():
-        to_row(r).wait_send()
+        total = given[1] + bottom[c]
+        for source in range(end):
+            br_copy(source).wait_recv()
+            total += bottom_row[source]
+        diag_ref[1] = total
 
     def drain(q, carry):
         def body(block, carry):
@@ -933,17 +1038,18 @@
             def _():
                 own_copy(q, (c + shift) % cols_axis).wait_send()
 
-        for t in range(groups):
-            pair_copy(q, t).wait_send()
-        for shift in range(1, groups):
-            group_copy(q, shift).wait_send()
         return carry
 
     lax.fori_loop(0, chunks, drain, 0)
-    for n in range(3):
-        each_column(lambda j: term_drain(n, j))
-        for shift in range(1, rows_axis):
-            tr_copy(n, (r + shift) % rows_axis).wait_send()
+    sums_sent(last - 1)
+    sums_sent(last)
+    each_column(lambda j: term_drain(0, j))
+    for n in (1, 2):
+        each_column(lambda j: term_drain(n, j), end)
+        each_row(n, lambda target: tr_copy(n, target).wait_send())
+    chain_drain()
+    late_drain()
+    each_column(bottom_drain)
 
 
 def fused(inverse_tile, panels, link_panel, given, tiles):
@@ -973,7 +1079,7 @@
             vmem((2, tile, depth), f32),
             vmem((rows, 2 * width), bf16),
             vmem((chunks, rows_axis, rows, width), f32),
-            vmem((chunks, cols_axis, rows, width), f32),
+            vmem((2, cols_axis, rows, width), f32),
             vmem((chunks, groups, rows, width), f32),
             vmem((chunks, max(groups - 1, 1), rows, width), f32),
             vmem((chunks, rows, width), f32),
@@ -1003,12 +1109,25 @@
             dma((3, max(groups - 1, 1))),
             dma((3, rows_axis)),
             dma((3, rows_axis)),
-            vmem((height, span), f32),
-            vmem((height, span), f32),
+            vmem((2, rows_axis, height, span), f32),
+            dma((2, rows_axis)),
+            dma((2, rows_axis)),
+            vmem((rows_axis, 2, height, span), f32),
+            vmem((rows_axis, 2, height, span), f32),
+            vmem((max(groups - 1, 1), rows_axis, 2, height, span), f32),
+            vmem((rows_axis, 2, height, span), f32),
+            dma((2,)),
+            dma,
+            dma((max(groups - 1, 1),)),
+            dma((rows_axis,)),
+            dma((rows_axis,)),
+            vmem((cols_axis, height, span), f32),
+            vmem((groups, height, span), f32),
             vmem((max(groups - 1, 1), height, span), f32),
             vmem((rows_axis, height, span), f32),
-            dma((2,)),
-            dma,
+            dma((cols_axis,)),
+            dma((cols_axis,)),
+            dma((cols_axis,)),
             dma((max(groups - 1, 1),)),
             dma,
             dma((rows_axis,)),

time: 198 us -> 184 us (0.929)
  Pallas kernels: 192 us -> 178 us
    pallas_call x1, Pallas kernels: 192 us -> 178 us  [fused(): pl.pallas_call(functools.partial(fused_kernel, (rows_axis, cols_axis)), o...]
where the time goes in v3:
time: 184 us; the launch traced here: 183 us
  Pallas kernels  178 us (97%)
  local copies, waits for them, and re-layouts  4.41 us (2%)
    pallas_call x1, Pallas kernels, fused(): pl.pallas_call(functools.partial(fused_kernel, (rows_axis, cols_axis)), o...  178 us
    unnamed x7, local copies, waits for them, and re-layouts  4.41 us

profile of v3, /device:TPU:3, one launch (start us, length us, event | category | flops | bytes accessed | tf_op | source)
XLA Modules:
  0.0 182.7 jit_solution(2002253879590838343)
XLA Ops:
  0.6 177.7 %shard_map.76 = (f32[2,512,512]{2,1,0:T(8,128)}, f32[2,128,128]{2,1,0:T(8,128)}, f32[128,128]{1,0:T(8,128)}) custom-call(s32[2,64]{1,0:T(2,128)} %bitcast.13, f32[2048,2048]{1,0:T(8,128)} %a_hbm.1, f32[2,512,512]{2,1,0:T(8,128)} %bitcast.7, f32[512,512]{1,0:T(8,128)} %bitcast.9, f32[2,128,128]{2,1,0:T(8,128)} %bitcast.10), custom_call_target="tpu_custom_call" | custom-call | tf_op jit(solution)/shard_map/pallas_call | solution.py:1067
  178.3 0.0 copy-start
  178.3 0.0 copy-start.1
  178.3 3.1 %copy.11 = f32[1,2,512,512]{3,2,1,0:T(8,128)} copy(f32[1,2,512,512]{3,2,1,0:T(8,128)} %bitcast.8) | data formatting | bytes 4194304
  181.4 0.0 copy-done
  181.4 0.7 copy.12
  182.1 0.0 copy-done.1
  182.1 0.6 copy.13
Async XLA Ops:
  178.3 3.1 %copy-start = (f32[2,128,128]{2,1,0:T(8,128)S(1)}, f32[2,128,128]{2,1,0:T(8,128)}, u32[]{:S(2)}) copy-start(f32[2,128,128]{2,1,0:T(8,128)} %get-tuple-element.7) | copy-start | bytes 393220
  178.3 3.8 %copy-start.1 = (f32[128,128]{1,0:T(8,128)S(1)}, f32[128,128]{1,0:T(8,128)}, u32[]{:S(2)}) copy-start(f32[128,128]{1,0:T(8,128)} %get-tuple-element.8) | copy-start | bytes 196612
